TPU v7x, 256 devices: a whole 4x4x8 slice. The times are simulated.
256 devices in a mesh: row: 16 (over z_hi, y, core), col: 16 (over x, z_lo).
Axes of the slice: x: 4, y: 4, z: 8 (z_hi: 2, z_lo: 4; z = z_hi * 4 + z_lo), core: 2. Of those that a mesh axis runs over, the one named last changes fastest.
Arguments:
- act_sketch: bfloat16 [2, 8192, 256], P(None, 'row'), may hold values from -6 to 6
- grad_sketch: bfloat16 [2, 8192, 256], P(None, 'row'), may hold values from -6 to 6
- targets: float32 [8192, 256], P('row'), may hold values from -6 to 6
Outputs:
- residual: float32 [8192, 256], P(('row', 'col'))
All inputs are finite; a program needn't handle non-finite values.
Results may differ from a plain program's by a relative error of at most 0.014.
The roundings to bfloat16 on the way count: a program that leaves them out, or rounds other values in their place, can miss the bound.
Values may be sent and summed in bfloat16 or wider, within the bound.
A program may use at most 64 MiB of HBM per device.

v0:
```python
import math
import jax
import jax.numpy as jnp
from jax import lax
from jax.sharding import PartitionSpec as P

ITERS = 8


def broadcast(value, axis, source):
    kept = jnp.where(lax.axis_index(axis) == source, value, 0).astype(value.dtype)
    return lax.psum(kept, axis)


def spread(panel, root):
    return broadcast(panel, "row", root)


def gram_pair(left, right):
    return lax.dot_general(
        left, right, (((1,), (1,)), ((), ())), preferred_element_type=jnp.float32
    )


def body(act_sketch, grad_sketch, targets):
    row_count = lax.axis_size("row")
    col_count = lax.axis_size("col")
    ratio = col_count // row_count
    examples = targets.shape[0]
    col_block = examples // ratio
    share_rows = examples // col_count
    col_place = lax.axis_index("col")
    root = col_place // ratio
    scale = act_sketch.shape[2] * math.sqrt(examples * row_count) / 4.0
    act_cols, grad_cols = (broadcast(act_sketch, "row", root), broadcast(grad_sketch, "row", root))
    total = jnp.zeros((examples, col_block), jnp.float32)
    for layer in range(act_sketch.shape[0]):
        act_gram = gram_pair(act_sketch[layer], act_cols[layer])
        grad_gram = gram_pair(grad_sketch[layer], grad_cols[layer])
        total = total + act_gram * grad_gram
    kernel = (total / scale).astype(jnp.bfloat16)
    share = lax.dynamic_slice_in_dim(targets, col_place * share_rows, share_rows, 0)
    for step in range(ITERS):
        squashed = jnp.tanh(share).astype(jnp.bfloat16)
        gathered = lax.all_gather(squashed, "col", axis=0, tiled=True)
        panel = spread(gathered, root)
        partial_value = jnp.dot(kernel, panel, preferred_element_type=jnp.float32)
        piece = lax.psum_scatter(partial_value, "col", scatter_dimension=0, tiled=True)
        share = share - 0.05 * piece
    return share


def solution(mesh):
    return jax.shard_map(
        body,
        mesh=mesh,
        in_specs=(P(None, "row", None), P(None, "row", None), P("row", None)),
        out_specs=P(("row", "col"), None),
        check_vma=False,
    )
```

profile of v0, /device:TPU:8, one launch (start us, length us, event | category | flops | bytes accessed | tf_op | source)
XLA Modules:
  0.0 2479.9 jit_solution(18417355909062240451)
XLA Ops:
  6.5 0.8 tanh_convert_fusion.7
  7.4 46.0 %all_gather.24 = bf16[512,256]{1,0:T(8,128)(2,1)S(1)} all-gather(bf16[32,256]{1,0:T(8,128)(2,1)S(1)} %tanh_convert_fusion.7), channel_id=1, replica_groups=mesh['row'=16,'col'=16] {'col'}, dimensions={0}, use_global_device_ids=true | all-gather | bytes 278528 | tf_op jit(solution)/shard_map/all_gather | solution.py:45
  53.3 0.7 broadcast_select_fusion.9
  54.0 1.1 broadcast_select_fusion
  55.2 172.0 %all-reduce.24.cloned.1.call-done = (bf16[2,512,256]{2,1,0:T(8,128)(2,1)}, bf16[2,512,256]{2,1,0:T(8,128)(2,1)}, bf16[512,256]{1,0:T(8,128)(2,1)}) async-done(((bf16[2,512,256]{2,1,0:T(8,128)(2,1)}, bf16[2,512,256]{2,1,0:T(8,128)(2,1)}, bf16[512,256]{1,0:T(8,128)(2,1)}), (bf16[2,512,256]{2,1,0:T(8,128)(2,1)}, bf16[2,512,256]{2,1,0:T(8,128)(2,1)}, bf16[512,256]{1,0:T(8,128)(2,1)})) %all-reduce.24.cloned.1.call-update) | async-done | bytes 1310736 | tf_op jit(solution)/shard_map/psum | solution.py:12
  227.2 1.3 fusion.3
  230.9 1.1 fusion.13
  232.1 94.1 %reduce-scatter.9.cloned.1.call-done = f32[32,256]{1,0:T(8,128)} async-done(((f32[512,256]{1,0:T(8,128)}), f32[32,256]{1,0:T(8,128)}) %reduce-scatter.9.cloned.1.call-update) | async-done | bytes 32784 | tf_op jit(solution)/shard_map/reduce_scatter | solution.py:48
  326.2 0.8 tanh_convert_fusion.6
  327.0 39.1 %all_gather.25 = bf16[512,256]{1,0:T(8,128)(2,1)S(1)} all-gather(bf16[32,256]{1,0:T(8,128)(2,1)S(1)} %get-tuple-element.12), channel_id=1, replica_groups=mesh['row'=16,'col'=16] {'col'}, dimensions={0}, use_global_device_ids=true | all-gather | bytes 278528 | tf_op jit(solution)/shard_map/all_gather | solution.py:45
  366.2 0.7 broadcast_select_fusion.8
  367.0 169.6 %all-reduce.10.cloned.1.call-done = bf16[512,256]{1,0:T(8,128)(2,1)} async-done(((bf16[512,256]{1,0:T(8,128)(2,1)}), bf16[512,256]{1,0:T(8,128)(2,1)}) %all-reduce.10.cloned.1.call-update) | async-done | bytes 262160 | tf_op jit(solution)/shard_map/psum | solution.py:12
  536.6 2.1 fusion.14
  538.7 94.2 %reduce-scatter.11.cloned.1.call-done = f32[32,256]{1,0:T(8,128)} async-done(((f32[512,256]{1,0:T(8,128)}), f32[32,256]{1,0:T(8,128)}) %reduce-scatter.11.cloned.1.call-update) | async-done | bytes 32784 | tf_op jit(solution)/shard_map/reduce_scatter | solution.py:48
  633.0 0.8 tanh_convert_fusion.5
  633.8 39.5 %all_gather.26 = bf16[512,256]{1,0:T(8,128)(2,1)S(1)} all-gather(bf16[32,256]{1,0:T(8,128)(2,1)S(1)} %tanh_convert_fusion.5), channel_id=1, replica_groups=mesh['row'=16,'col'=16] {'col'}, dimensions={0}, use_global_device_ids=true | all-gather | bytes 278528 | tf_op jit(solution)/shard_map/all_gather | solution.py:45
  673.2 0.7 broadcast_select_fusion.7
  674.0 169.0 %all-reduce.12.cloned.1.call-done = bf16[512,256]{1,0:T(8,128)(2,1)} async-done(((bf16[512,256]{1,0:T(8,128)(2,1)}), bf16[512,256]{1,0:T(8,128)(2,1)}) %all-reduce.12.cloned.1.call-update) | async-done | bytes 262160 | tf_op jit(solution)/shard_map/psum | solution.py:12
  843.0 2.1 fusion.15
  845.2 94.2 %reduce-scatter.13.cloned.1.call-done = f32[32,256]{1,0:T(8,128)} async-done(((f32[512,256]{1,0:T(8,128)}), f32[32,256]{1,0:T(8,128)}) %reduce-scatter.13.cloned.1.call-update) | async-done | bytes 32784 | tf_op jit(solution)/shard_map/reduce_scatter | solution.py:48
  939.4 0.8 tanh_convert_fusion.4
  940.2 39.5 %all_gather.27 = bf16[512,256]{1,0:T(8,128)(2,1)S(1)} all-gather(bf16[32,256]{1,0:T(8,128)(2,1)S(1)} %get-tuple-element.10), channel_id=1, replica_groups=mesh['row'=16,'col'=16] {'col'}, dimensions={0}, use_global_device_ids=true | all-gather | bytes 278528 | tf_op jit(solution)/shard_map/all_gather | solution.py:45
  979.7 0.7 broadcast_select_fusion.6
  980.5 169.0 %all-reduce.14.cloned.1.call-done = bf16[512,256]{1,0:T(8,128)(2,1)} async-done(((bf16[512,256]{1,0:T(8,128)(2,1)}), bf16[512,256]{1,0:T(8,128)(2,1)}) %all-reduce.14.cloned.1.call-update) | async-done | bytes 262160 | tf_op jit(solution)/shard_map/psum | solution.py:12
  1149.5 2.1 fusion.16
  1151.6 94.4 %reduce-scatter.15.cloned.1.call-done = f32[32,256]{1,0:T(8,128)} async-done(((f32[512,256]{1,0:T(8,128)}), f32[32,256]{1,0:T(8,128)}) %reduce-scatter.15.cloned.1.call-update) | async-done | bytes 32784 | tf_op jit(solution)/shard_map/reduce_scatter | solution.py:48
  1246.1 0.8 tanh_convert_fusion.3
  1246.8 39.5 %all_gather.28 = bf16[512,256]{1,0:T(8,128)(2,1)S(1)} all-gather(bf16[32,256]{1,0:T(8,128)(2,1)S(1)} %tanh_convert_fusion.3), channel_id=1, replica_groups=mesh['row'=16,'col'=16] {'col'}, dimensions={0}, use_global_device_ids=true | all-gather | bytes 278528 | tf_op jit(solution)/shard_map/all_gather | solution.py:45
  1286.3 0.7 broadcast_select_fusion.5
  1287.1 169.2 %all-reduce.16.cloned.1.call-done = bf16[512,256]{1,0:T(8,128)(2,1)} async-done(((bf16[512,256]{1,0:T(8,128)(2,1)}), bf16[512,256]{1,0:T(8,128)(2,1)}) %all-reduce.16.cloned.1.call-update) | async-done | bytes 262160 | tf_op jit(solution)/shard_map/psum | solution.py:12
  1456.3 2.1 fusion.17
  1458.5 94.2 %reduce-scatter.17.cloned.1.call-done = f32[32,256]{1,0:T(8,128)} async-done(((f32[512,256]{1,0:T(8,128)}), f32[32,256]{1,0:T(8,128)}) %reduce-scatter.17.cloned.1.call-update) | async-done | bytes 32784 | tf_op jit(solution)/shard_map/reduce_scatter | solution.py:48
  1552.7 0.8 tanh_convert_fusion.2
  1553.5 39.5 %all_gather.29 = bf16[512,256]{1,0:T(8,128)(2,1)S(1)} all-gather(bf16[32,256]{1,0:T(8,128)(2,1)S(1)} %get-tuple-element.8), channel_id=1, replica_groups=mesh['row'=16,'col'=16] {'col'}, dimensions={0}, use_global_device_ids=true | all-gather | bytes 278528 | tf_op jit(solution)/shard_map/all_gather | solution.py:45
  1593.7 169.0 %all-reduce.18.cloned.1.call-done = bf16[512,256]{1,0:T(8,128)(2,1)} async-done(((bf16[512,256]{1,0:T(8,128)(2,1)}), bf16[512,256]{1,0:T(8,128)(2,1)}) %all-reduce.18.cloned.1.call-update) | async-done | bytes 262160 | tf_op jit(solution)/shard_map/psum | solution.py:12
  1762.8 2.1 fusion.18
  1764.9 94.2 %reduce-scatter.19.cloned.1.call-done = f32[32,256]{1,0:T(8,128)} async-done(((f32[512,256]{1,0:T(8,128)}), f32[32,256]{1,0:T(8,128)}) %reduce-scatter.19.cloned.1.call-update) | async-done | bytes 32784 | tf_op jit(solution)/shard_map/reduce_scatter | solution.py:48
  1859.2 0.8 tanh_convert_fusion.1
  1859.9 39.5 %all_gather.30 = bf16[512,256]{1,0:T(8,128)(2,1)S(1)} all-gather(bf16[32,256]{1,0:T(8,128)(2,1)S(1)} %tanh_convert_fusion.1), channel_id=1, replica_groups=mesh['row'=16,'col'=16] {'col'}, dimensions={0}, use_global_device_ids=true | all-gather | bytes 278528 | tf_op jit(solution)/shard_map/all_gather | solution.py:45
  1900.2 169.0 %all-reduce.20.cloned.1.call-done = bf16[512,256]{1,0:T(8,128)(2,1)} async-done(((bf16[512,256]{1,0:T(8,128)(2,1)}), bf16[512,256]{1,0:T(8,128)(2,1)}) %all-reduce.20.cloned.1.call-update) | async-done | bytes 262160 | tf_op jit(solution)/shard_map/psum | solution.py:12
  2069.2 2.1 fusion.19
  2071.4 94.2 %reduce-scatter.21.cloned.1.call-done = f32[32,256]{1,0:T(8,128)} async-done(((f32[512,256]{1,0:T(8,128)}), f32[32,256]{1,0:T(8,128)}) %reduce-scatter.21.cloned.1.call-update) | async-done | bytes 32784 | tf_op jit(solution)/shard_map/reduce_scatter | solution.py:48
  2165.6 0.8 tanh_convert_fusion
  2166.4 39.5 %all_gather.31 = bf16[512,256]{1,0:T(8,128)(2,1)S(1)} all-gather(bf16[32,256]{1,0:T(8,128)(2,1)S(1)} %tanh_convert_fusion), channel_id=1, replica_groups=mesh['row'=16,'col'=16] {'col'}, dimensions={0}, use_global_device_ids=true | all-gather | bytes 278528 | tf_op jit(solution)/shard_map/all_gather | solution.py:45
  2206.6 169.0 %all-reduce.22.cloned.1.call-done = bf16[512,256]{1,0:T(8,128)(2,1)} async-done(((bf16[512,256]{1,0:T(8,128)(2,1)}), bf16[512,256]{1,0:T(8,128)(2,1)}) %all-reduce.22.cloned.1.call-update) | async-done | bytes 262160 | tf_op jit(solution)/shard_map/psum | solution.py:12
  2375.7 2.1 fusion.20
  2377.8 94.2 %reduce-scatter.23.cloned.1.call-done = f32[32,256]{1,0:T(8,128)} async-done(((f32[512,256]{1,0:T(8,128)}), f32[32,256]{1,0:T(8,128)}) %reduce-scatter.23.cloned.1.call-update) | async-done | bytes 32784 | tf_op jit(solution)/shard_map/reduce_scatter | solution.py:48
  2472.0 1.4 multiply_subtract_fusion
  (56 shorter events, 5.4 us)
Async XLA Ops:
  6.5 47.5 %copy-start = (bf16[2,512,256]{2,1,0:T(8,128)(2,1)S(1)}, bf16[2,512,256]{2,1,0:T(8,128)(2,1)}, u32[]{:S(2)}) copy-start(bf16[2,512,256]{2,1,0:T(8,128)(2,1)} %param.4) | copy-start | bytes 1572868
  6.5 220.7 %all-reduce.24.cloned.1.call-start = ((), (), s32[]{:S(2)}) async-start(), calls=%async_computation.23 | async-start | bytes 2621440 | tf_op jit(solution)/shard_map/psum | solution.py:12
  55.1 172.1 %copy-start.1 = (bf16[2,512,256]{2,1,0:T(8,128)(2,1)S(1)}, bf16[2,512,256]{2,1,0:T(8,128)(2,1)}, u32[]{:S(2)}) copy-start(bf16[2,512,256]{2,1,0:T(8,128)(2,1)} %param.3) | copy-start | bytes 1572868
  55.1 271.1 %reduce-scatter.9.cloned.1.call-start = ((), (), s32[]{:S(2)}) async-start(), calls=%async_computation.8 | async-start | bytes 557056 | tf_op jit(solution)/shard_map/reduce_scatter | solution.py:48
  227.2 1.4 copy-start.3
  228.6 1.0 copy-start.2
  230.0 1.0 copy-start.5
  232.1 304.5 %all-reduce.10.cloned.1.call-start = ((), (), s32[]{:S(2)}) async-start(), calls=%async_computation.9 | async-start | bytes 524288 | tf_op jit(solution)/shard_map/psum | solution.py:12
  366.9 266.1 %reduce-scatter.11.cloned.1.call-start = ((), (), s32[]{:S(2)}) async-start(), calls=%async_computation.10 | async-start | bytes 557056 | tf_op jit(solution)/shard_map/reduce_scatter | solution.py:48
  538.7 304.3 %all-reduce.12.cloned.1.call-start = ((), (), s32[]{:S(2)}) async-start(), calls=%async_computation.11 | async-start | bytes 524288 | tf_op jit(solution)/shard_map/psum | solution.py:12
  674.0 265.5 %reduce-scatter.13.cloned.1.call-start = ((), (), s32[]{:S(2)}) async-start(), calls=%async_computation.12 | async-start | bytes 557056 | tf_op jit(solution)/shard_map/reduce_scatter | solution.py:48
  845.1 94.3 %copy-start.7 = (f32[32,256]{1,0:T(8,128)S(1)}, f32[32,256]{1,0:T(8,128)}, u32[]{:S(2)}) copy-start(f32[32,256]{1,0:T(8,128)} %reduce-scatter.11.cloned.1.call-done) | copy-start | bytes 98308
  845.1 304.4 %all-reduce.14.cloned.1.call-start = ((), (), s32[]{:S(2)}) async-start(), calls=%async_computation.13 | async-start | bytes 524288 | tf_op jit(solution)/shard_map/psum | solution.py:12
  980.4 265.6 %reduce-scatter.15.cloned.1.call-start = ((), (), s32[]{:S(2)}) async-start(), calls=%async_computation.14 | async-start | bytes 557056 | tf_op jit(solution)/shard_map/reduce_scatter | solution.py:48
  1151.6 304.7 %all-reduce.16.cloned.1.call-start = ((), (), s32[]{:S(2)}) async-start(), calls=%async_computation.15 | async-start | bytes 524288 | tf_op jit(solution)/shard_map/psum | solution.py:12
  1287.1 265.7 %reduce-scatter.17.cloned.1.call-start = ((), (), s32[]{:S(2)}) async-start(), calls=%async_computation.16 | async-start | bytes 557056 | tf_op jit(solution)/shard_map/reduce_scatter | solution.py:48
  1458.4 94.3 %copy-start.8 = (f32[32,256]{1,0:T(8,128)S(1)}, f32[32,256]{1,0:T(8,128)}, u32[]{:S(2)}) copy-start(f32[32,256]{1,0:T(8,128)} %reduce-scatter.15.cloned.1.call-done) | copy-start | bytes 98308
  1458.4 304.3 %all-reduce.18.cloned.1.call-start = ((), (), s32[]{:S(2)}) async-start(), calls=%async_computation.17 | async-start | bytes 524288 | tf_op jit(solution)/shard_map/psum | solution.py:12
  1593.7 265.5 %reduce-scatter.19.cloned.1.call-start = ((), (), s32[]{:S(2)}) async-start(), calls=%async_computation.18 | async-start | bytes 557056 | tf_op jit(solution)/shard_map/reduce_scatter | solution.py:48
  1764.9 304.3 %all-reduce.20.cloned.1.call-start = ((), (), s32[]{:S(2)}) async-start(), calls=%async_computation.19 | async-start | bytes 524288 | tf_op jit(solution)/shard_map/psum | solution.py:12
  1900.1 265.5 %reduce-scatter.21.cloned.1.call-start = ((), (), s32[]{:S(2)}) async-start(), calls=%async_computation.20 | async-start | bytes 557056 | tf_op jit(solution)/shard_map/reduce_scatter | solution.py:48
  2071.3 94.3 %copy-start.4 = (f32[32,256]{1,0:T(8,128)S(1)}, f32[32,256]{1,0:T(8,128)}, u32[]{:S(2)}) copy-start(f32[32,256]{1,0:T(8,128)} %reduce-scatter.19.cloned.1.call-done) | copy-start | bytes 98308
  2071.3 304.3 %all-reduce.22.cloned.1.call-start = ((), (), s32[]{:S(2)}) async-start(), calls=%async_computation.21 | async-start | bytes 524288 | tf_op jit(solution)/shard_map/psum | solution.py:12
  2206.6 265.4 %reduce-scatter.23.cloned.1.call-start = ((), (), s32[]{:S(2)}) async-start(), calls=%async_computation.22 | async-start | bytes 557056 | tf_op jit(solution)/shard_map/reduce_scatter | solution.py:48
  2377.7 94.2 %copy-start.6 = (f32[32,256]{1,0:T(8,128)S(1)}, f32[32,256]{1,0:T(8,128)}, u32[]{:S(2)}) copy-start(f32[32,256]{1,0:T(8,128)} %reduce-scatter.21.cloned.1.call-done) | copy-start | bytes 98308
Sparse Core Ops, SparseCore 0:
  55.3 171.9 all-reduce.23
  232.2 93.9 reduce-scatter.8
  367.0 169.5 all-reduce.9
  538.9 93.9 reduce-scatter.10
  674.1 168.9 all-reduce.11
  845.4 93.9 reduce-scatter.12
  980.5 168.9 all-reduce.13
  1152.0 94.0 reduce-scatter.14
  1287.2 169.1 all-reduce.15
  1458.7 93.9 reduce-scatter.16
  1593.8 168.9 all-reduce.17
  1765.1 93.9 reduce-scatter.18
  1900.3 168.9 all-reduce.19
  2071.6 93.9 reduce-scatter.20
  2206.7 168.9 all-reduce.21
  2378.0 93.9 reduce-scatter.22
where the time goes:
time: 2480 us
  waiting for transfers between devices  2110 us (85%)
  blocking collectives  322 us (13%)
    psum x8, waiting for transfers between devices, broadcast(): return lax.psum(kept, axis)  1360 us
    reduce_scatter x8, waiting for transfers between devices, body(): lax.psum_scatter(partial_value, 'col', scatter_dimension=0, tiled=True)  754 us
    all_gather x8, blocking collectives, body(): gathered = lax.all_gather(squashed, 'col', axis=0, tiled=True)  322 us
  transfers between devices with their start and end apart: 16, of which 16 were waited for; matrix products, arithmetic and copies ran while one was open for 0% of the time, Pallas kernels for 0%

commit v1 on v0

--- a/solution.py
+++ b/solution.py
@@ -42,7 +42,10 @@
     share = lax.dynamic_slice_in_dim(targets, col_place * share_rows, share_rows, 0)
     for step in range(ITERS):
         squashed = jnp.tanh(share).astype(jnp.bfloat16)
-        gathered = lax.all_gather(squashed, "col", axis=0, tiled=True)
+        gathered = jnp.concatenate(
+            lax.all_to_all(jnp.stack([squashed] * lax.axis_size("col"), axis=0), "col", 0, 0),
+            axis=0,
+        )
         panel = spread(gathered, root)
         partial_value = jnp.dot(kernel, panel, preferred_element_type=jnp.float32)
         piece = lax.psum_scatter(partial_value, "col", scatter_dimension=0, tiled=True)

time: 2480 us -> 2260 us (0.911)
  blocking collectives: 322 us -> 82.2 us
    all_gather x8 -> x0, blocking collectives: 322 us -> none  [body(): gathered = lax.all_gather(squashed, 'col', axis=0, tiled=True)]
    all_to_all x0 -> x7, blocking collectives: none -> 82.2 us  [body(): lax.all_to_all(jnp.stack([squashed] * lax.axis_size('col'), axis=0), 'col...]
  transfers between devices with their start and end apart: 16 -> 17, of which waited for: 16 -> 17; matrix products, arithmetic and copies ran while one was open for 0% -> 0% of each run, Pallas kernels for 0% -> 0%
where the time goes in v1:
time: 2260 us
  waiting for transfers between devices  2120 us (94%)
  blocking collectives  82.2 us (4%)
    psum x8, waiting for transfers between devices, broadcast(): return lax.psum(kept, axis)  1360 us
    reduce_scatter x8, waiting for transfers between devices, body(): lax.psum_scatter(partial_value, 'col', scatter_dimension=0, tiled=True)  754 us
    all_to_all x7, blocking collectives, body(): lax.all_to_all(jnp.stack([squashed] * lax.axis_size('col'), axis=0), 'col...  82.2 us
  transfers between devices with their start and end apart: 17, of which 17 were waited for; matrix products, arithmetic and copies ran while one was open for 0% of the time, Pallas kernels for 0%

profile of v1, /device:TPU:8, one launch (start us, length us, event | category | flops | bytes accessed | tf_op | source)
XLA Modules:
  0.0 2259.5 jit_solution(14603944613635490401)
XLA Ops:
  6.5 0.8 tanh_convert_fusion.7
  7.4 0.7 stack.16
  8.1 8.5 all-to-all-start
  16.6 1.1 broadcast_select_fusion
  17.7 9.7 all-to-all-done
  27.5 0.7 broadcast_select_fusion.9
  28.3 172.4 %all-reduce.24.cloned.1.call-done = (bf16[2,512,256]{2,1,0:T(8,128)(2,1)}, bf16[2,512,256]{2,1,0:T(8,128)(2,1)}, bf16[512,256]{1,0:T(8,128)(2,1)}) async-done(((bf16[2,512,256]{2,1,0:T(8,128)(2,1)}, bf16[2,512,256]{2,1,0:T(8,128)(2,1)}, bf16[512,256]{1,0:T(8,128)(2,1)}), (bf16[2,512,256]{2,1,0:T(8,128)(2,1)}, bf16[2,512,256]{2,1,0:T(8,128)(2,1)}, bf16[512,256]{1,0:T(8,128)(2,1)})) %all-reduce.24.cloned.1.call-update) | async-done | bytes 1310736 | tf_op jit(solution)/shard_map/psum | solution.py:12
  200.7 1.3 fusion.3
  204.4 1.1 fusion.13
  205.6 94.1 %reduce-scatter.9.cloned.1.call-done = f32[32,256]{1,0:T(8,128)} async-done(((f32[512,256]{1,0:T(8,128)}), f32[32,256]{1,0:T(8,128)}) %reduce-scatter.9.cloned.1.call-update) | async-done | bytes 32784 | tf_op jit(solution)/shard_map/reduce_scatter | solution.py:51
  299.7 0.8 tanh_convert_fusion.6
  300.5 11.7 all_to_all.40
  312.3 0.7 broadcast_select_fusion.8
  313.1 169.1 %all-reduce.10.cloned.1.call-done = bf16[512,256]{1,0:T(8,128)(2,1)} async-done(((bf16[512,256]{1,0:T(8,128)(2,1)}), bf16[512,256]{1,0:T(8,128)(2,1)}) %all-reduce.10.cloned.1.call-update) | async-done | bytes 262160 | tf_op jit(solution)/shard_map/psum | solution.py:12
  482.2 2.1 fusion.14
  484.3 94.2 %reduce-scatter.11.cloned.1.call-done = f32[32,256]{1,0:T(8,128)} async-done(((f32[512,256]{1,0:T(8,128)}), f32[32,256]{1,0:T(8,128)}) %reduce-scatter.11.cloned.1.call-update) | async-done | bytes 32784 | tf_op jit(solution)/shard_map/reduce_scatter | solution.py:51
  578.5 0.8 tanh_convert_fusion.5
  579.3 11.7 all_to_all.41
  591.9 169.1 %all-reduce.12.cloned.1.call-done = bf16[512,256]{1,0:T(8,128)(2,1)} async-done(((bf16[512,256]{1,0:T(8,128)(2,1)}), bf16[512,256]{1,0:T(8,128)(2,1)}) %all-reduce.12.cloned.1.call-update) | async-done | bytes 262160 | tf_op jit(solution)/shard_map/psum | solution.py:12
  761.0 2.1 fusion.15
  763.1 94.2 %reduce-scatter.13.cloned.1.call-done = f32[32,256]{1,0:T(8,128)} async-done(((f32[512,256]{1,0:T(8,128)}), f32[32,256]{1,0:T(8,128)}) %reduce-scatter.13.cloned.1.call-update) | async-done | bytes 32784 | tf_op jit(solution)/shard_map/reduce_scatter | solution.py:51
  857.4 0.8 tanh_convert_fusion.4
  858.2 11.7 all_to_all.42
  869.9 0.7 broadcast_select_fusion.6
  870.7 169.1 %all-reduce.14.cloned.1.call-done = bf16[512,256]{1,0:T(8,128)(2,1)} async-done(((bf16[512,256]{1,0:T(8,128)(2,1)}), bf16[512,256]{1,0:T(8,128)(2,1)}) %all-reduce.14.cloned.1.call-update) | async-done | bytes 262160 | tf_op jit(solution)/shard_map/psum | solution.py:12
  1039.8 2.1 fusion.16
  1042.0 94.4 %reduce-scatter.15.cloned.1.call-done = f32[32,256]{1,0:T(8,128)} async-done(((f32[512,256]{1,0:T(8,128)}), f32[32,256]{1,0:T(8,128)}) %reduce-scatter.15.cloned.1.call-update) | async-done | bytes 32784 | tf_op jit(solution)/shard_map/reduce_scatter | solution.py:51
  1136.3 0.8 tanh_convert_fusion.3
  1137.1 11.7 all_to_all.43
  1149.7 169.1 %all-reduce.16.cloned.1.call-done = bf16[512,256]{1,0:T(8,128)(2,1)} async-done(((bf16[512,256]{1,0:T(8,128)(2,1)}), bf16[512,256]{1,0:T(8,128)(2,1)}) %all-reduce.16.cloned.1.call-update) | async-done | bytes 262160 | tf_op jit(solution)/shard_map/psum | solution.py:12
  1318.8 2.1 fusion.17
  1321.0 94.2 %reduce-scatter.17.cloned.1.call-done = f32[32,256]{1,0:T(8,128)} async-done(((f32[512,256]{1,0:T(8,128)}), f32[32,256]{1,0:T(8,128)}) %reduce-scatter.17.cloned.1.call-update) | async-done | bytes 32784 | tf_op jit(solution)/shard_map/reduce_scatter | solution.py:51
  1415.2 0.8 tanh_convert_fusion.2
  1416.0 11.7 all_to_all.44
  1428.5 169.1 %all-reduce.18.cloned.1.call-done = bf16[512,256]{1,0:T(8,128)(2,1)} async-done(((bf16[512,256]{1,0:T(8,128)(2,1)}), bf16[512,256]{1,0:T(8,128)(2,1)}) %all-reduce.18.cloned.1.call-update) | async-done | bytes 262160 | tf_op jit(solution)/shard_map/psum | solution.py:12
  1597.7 2.1 fusion.18
  1599.8 94.2 %reduce-scatter.19.cloned.1.call-done = f32[32,256]{1,0:T(8,128)} async-done(((f32[512,256]{1,0:T(8,128)}), f32[32,256]{1,0:T(8,128)}) %reduce-scatter.19.cloned.1.call-update) | async-done | bytes 32784 | tf_op jit(solution)/shard_map/reduce_scatter | solution.py:51
  1694.0 0.8 tanh_convert_fusion.1
  1694.8 11.7 all_to_all.45
  1707.4 169.1 %all-reduce.20.cloned.1.call-done = bf16[512,256]{1,0:T(8,128)(2,1)} async-done(((bf16[512,256]{1,0:T(8,128)(2,1)}), bf16[512,256]{1,0:T(8,128)(2,1)}) %all-reduce.20.cloned.1.call-update) | async-done | bytes 262160 | tf_op jit(solution)/shard_map/psum | solution.py:12
  1876.5 2.1 fusion.19
  1878.6 94.2 %reduce-scatter.21.cloned.1.call-done = f32[32,256]{1,0:T(8,128)} async-done(((f32[512,256]{1,0:T(8,128)}), f32[32,256]{1,0:T(8,128)}) %reduce-scatter.21.cloned.1.call-update) | async-done | bytes 32784 | tf_op jit(solution)/shard_map/reduce_scatter | solution.py:51
  1972.9 0.8 tanh_convert_fusion
  1973.7 11.7 all_to_all.46
  1986.2 169.1 %all-reduce.22.cloned.1.call-done = bf16[512,256]{1,0:T(8,128)(2,1)} async-done(((bf16[512,256]{1,0:T(8,128)(2,1)}), bf16[512,256]{1,0:T(8,128)(2,1)}) %all-reduce.22.cloned.1.call-update) | async-done | bytes 262160 | tf_op jit(solution)/shard_map/psum | solution.py:12
  2155.3 2.1 fusion.20
  2157.4 94.2 %reduce-scatter.23.cloned.1.call-done = f32[32,256]{1,0:T(8,128)} async-done(((f32[512,256]{1,0:T(8,128)}), f32[32,256]{1,0:T(8,128)}) %reduce-scatter.23.cloned.1.call-update) | async-done | bytes 32784 | tf_op jit(solution)/shard_map/reduce_scatter | solution.py:51
  2251.6 1.4 multiply_subtract_fusion
  (65 shorter events, 6.9 us)
Async XLA Ops:
  6.5 10.1 copy-start
  8.1 19.4 all-to-all-start
  16.6 184.1 %all-reduce.24.cloned.1.call-start = ((), (), s32[]{:S(2)}) async-start(), calls=%async_computation.31 | async-start | bytes 2621440 | tf_op jit(solution)/shard_map/psum | solution.py:12
  28.2 172.5 %copy-start.1 = (bf16[2,512,256]{2,1,0:T(8,128)(2,1)S(1)}, bf16[2,512,256]{2,1,0:T(8,128)(2,1)}, u32[]{:S(2)}) copy-start(bf16[2,512,256]{2,1,0:T(8,128)(2,1)} %param.3) | copy-start | bytes 1572868
  28.2 271.5 %reduce-scatter.9.cloned.1.call-start = ((), (), s32[]{:S(2)}) async-start(), calls=%async_computation.16 | async-start | bytes 557056 | tf_op jit(solution)/shard_map/reduce_scatter | solution.py:51
  200.7 1.4 copy-start.3
  202.1 1.0 copy-start.2
  203.4 1.0 copy-start.5
  205.5 276.6 %all-reduce.10.cloned.1.call-start = ((), (), s32[]{:S(2)}) async-start(), calls=%async_computation.17 | async-start | bytes 524288 | tf_op jit(solution)/shard_map/psum | solution.py:12
  313.0 265.5 %reduce-scatter.11.cloned.1.call-start = ((), (), s32[]{:S(2)}) async-start(), calls=%async_computation.18 | async-start | bytes 557056 | tf_op jit(solution)/shard_map/reduce_scatter | solution.py:51
  484.3 276.7 %all-reduce.12.cloned.1.call-start = ((), (), s32[]{:S(2)}) async-start(), calls=%async_computation.19 | async-start | bytes 524288 | tf_op jit(solution)/shard_map/psum | solution.py:12
  591.8 265.6 %reduce-scatter.13.cloned.1.call-start = ((), (), s32[]{:S(2)}) async-start(), calls=%async_computation.20 | async-start | bytes 557056 | tf_op jit(solution)/shard_map/reduce_scatter | solution.py:51
  763.1 94.3 %copy-start.7 = (f32[32,256]{1,0:T(8,128)S(1)}, f32[32,256]{1,0:T(8,128)}, u32[]{:S(2)}) copy-start(f32[32,256]{1,0:T(8,128)} %reduce-scatter.11.cloned.1.call-done) | copy-start | bytes 98308
  763.1 276.7 %all-reduce.14.cloned.1.call-start = ((), (), s32[]{:S(2)}) async-start(), calls=%async_computation.21 | async-start | bytes 524288 | tf_op jit(solution)/shard_map/psum | solution.py:12
  870.7 265.7 %reduce-scatter.15.cloned.1.call-start = ((), (), s32[]{:S(2)}) async-start(), calls=%async_computation.22 | async-start | bytes 557056 | tf_op jit(solution)/shard_map/reduce_scatter | solution.py:51
  1041.9 276.9 %all-reduce.16.cloned.1.call-start = ((), (), s32[]{:S(2)}) async-start(), calls=%async_computation.23 | async-start | bytes 524288 | tf_op jit(solution)/shard_map/psum | solution.py:12
  1149.6 265.6 %reduce-scatter.17.cloned.1.call-start = ((), (), s32[]{:S(2)}) async-start(), calls=%async_computation.24 | async-start | bytes 557056 | tf_op jit(solution)/shard_map/reduce_scatter | solution.py:51
  1320.9 94.3 %copy-start.8 = (f32[32,256]{1,0:T(8,128)S(1)}, f32[32,256]{1,0:T(8,128)}, u32[]{:S(2)}) copy-start(f32[32,256]{1,0:T(8,128)} %reduce-scatter.15.cloned.1.call-done) | copy-start | bytes 98308
  1320.9 276.7 %all-reduce.18.cloned.1.call-start = ((), (), s32[]{:S(2)}) async-start(), calls=%async_computation.25 | async-start | bytes 524288 | tf_op jit(solution)/shard_map/psum | solution.py:12
  1428.5 265.6 %reduce-scatter.19.cloned.1.call-start = ((), (), s32[]{:S(2)}) async-start(), calls=%async_computation.26 | async-start | bytes 557056 | tf_op jit(solution)/shard_map/reduce_scatter | solution.py:51
  1599.8 276.7 %all-reduce.20.cloned.1.call-start = ((), (), s32[]{:S(2)}) async-start(), calls=%async_computation.27 | async-start | bytes 524288 | tf_op jit(solution)/shard_map/psum | solution.py:12
  1707.3 265.6 %reduce-scatter.21.cloned.1.call-start = ((), (), s32[]{:S(2)}) async-start(), calls=%async_computation.28 | async-start | bytes 557056 | tf_op jit(solution)/shard_map/reduce_scatter | solution.py:51
  1878.6 94.3 %copy-start.4 = (f32[32,256]{1,0:T(8,128)S(1)}, f32[32,256]{1,0:T(8,128)}, u32[]{:S(2)}) copy-start(f32[32,256]{1,0:T(8,128)} %reduce-scatter.19.cloned.1.call-done) | copy-start | bytes 98308
  1878.6 276.7 %all-reduce.22.cloned.1.call-start = ((), (), s32[]{:S(2)}) async-start(), calls=%async_computation.29 | async-start | bytes 524288 | tf_op jit(solution)/shard_map/psum | solution.py:12
  1986.2 265.5 %reduce-scatter.23.cloned.1.call-start = ((), (), s32[]{:S(2)}) async-start(), calls=%async_computation.30 | async-start | bytes 557056 | tf_op jit(solution)/shard_map/reduce_scatter | solution.py:51
  2157.4 94.2 %copy-start.6 = (f32[32,256]{1,0:T(8,128)S(1)}, f32[32,256]{1,0:T(8,128)}, u32[]{:S(2)}) copy-start(f32[32,256]{1,0:T(8,128)} %reduce-scatter.21.cloned.1.call-done) | copy-start | bytes 98308
Sparse Core Ops, SparseCore 0:
  28.3 172.2 all-reduce.23
  205.7 94.0 reduce-scatter.8
  313.1 168.9 all-reduce.9
  484.5 93.9 reduce-scatter.10
  591.9 169.0 all-reduce.11
  763.3 93.9 reduce-scatter.12
  870.8 169.0 all-reduce.13
  1042.3 93.9 reduce-scatter.14
  1149.7 169.0 all-reduce.15
  1321.1 93.9 reduce-scatter.16
  1428.6 169.0 all-reduce.17
  1600.0 93.9 reduce-scatter.18
  1707.4 169.0 all-reduce.19
  1878.8 93.9 reduce-scatter.20
  1986.3 169.0 all-reduce.21
  2157.7 93.9 reduce-scatter.22
